TPU v7x, 32 devices: a whole 2x2x4 slice. The times are simulated.
32 devices in a mesh: field: 4 (over y, x), gz: 8 (over z, core).
Axes of the slice: x: 2, y: 2, z: 4, core: 2. Of those that a mesh axis runs over, the one named last changes fastest.
Arguments:
- fields: bfloat16 [2048, 2, 8, 16, 256], P('gz', None, 'field'), may hold values from -8 to 8
- shells: int32 [2048, 16, 256], P('gz'), may hold values from 0 to 255
- mubins: int32 [2048, 16, 256], P('gz'), may hold values from 0 to 7, as said below
Outputs:
- power: float32 [3, 8, 256], replicated
Inputs may be any that keep to these rules, and one draw needn't show every extreme that they name: `mubins`: A cell's mu-bin index is never above its k-shell index.
All inputs are finite; a program needn't handle non-finite values.
Results may differ from a plain program's by a relative error of at most 0.00052.
Values may be sent and summed in bfloat16 or wider, within the bound.
A program may use at most 192 MiB of HBM per device.

v0:
```python
import math

import jax
import jax.numpy as jnp
import numpy as np
from jax import lax
from jax.sharding import PartitionSpec as P

NZ = 2048
SHELLS = 256
MUBINS = 8


def broadcast(value, axis, source):
    kept = jnp.where(lax.axis_index(axis) == source, value, 0).astype(value.dtype)
    return lax.psum(kept, axis)


def make_coef():
    table = np.zeros((3, 8, 7), np.float32)
    table[0, 0, 0] = 1.0
    table[1, 1, 0] = 1.0
    table[2, 1, 0] = -0.5
    table[2, 2, 1] = 1.5
    table[2, 3, 2] = 1.5
    table[2, 4, 3] = 1.5
    table[2, 5, 4] = 3.0
    table[2, 6, 5] = 3.0
    table[2, 7, 6] = 3.0
    return table


def dft_tables(length):
    index = jnp.arange(length, dtype=jnp.int32)
    product = index[:, None] * index[None, :] % length
    angle = product.astype(jnp.float32) * (2.0 * math.pi / length)
    factor = 1.0 / math.sqrt(length)
    return (
        (jnp.cos(angle) * factor).astype(jnp.bfloat16),
        (jnp.sin(angle) * factor).astype(jnp.bfloat16),
    )


def transform(lines, cos_table, sin_table):
    length, _, items, columns = lines.shape
    flat = lines.reshape(length, 2 * items * columns)
    first = jnp.dot(cos_table, flat, preferred_element_type=jnp.float32).reshape(
        length, 2, items, columns
    )
    second = jnp.dot(sin_table, flat, preferred_element_type=jnp.float32).reshape(
        length, 2, items, columns
    )
    real_part = first[:, 0] + second[:, 1]
    imag_part = first[:, 1] - second[:, 0]
    return jnp.stack([real_part, imag_part], axis=1)


def monomials(wave_x, wave_y, wave_z):
    square = wave_x * wave_x + wave_y * wave_y + wave_z * wave_z
    ones = jnp.ones_like(square)
    return jnp.stack(
        [
            ones,
            wave_x * wave_x / square,
            wave_y * wave_y / square,
            wave_z * wave_z / square,
            wave_x * wave_y / square,
            wave_x * wave_z / square,
            wave_y * wave_z / square,
        ]
    )


def bin_cells(values, shell_ids, mu_ids):
    cells = values.shape[1]
    block = math.gcd(cells, 32768)
    blocks = cells // block
    value_blocks = values.reshape(3, blocks, block).transpose(1, 0, 2)
    shell_blocks = shell_ids.reshape(blocks, block)
    mu_blocks = mu_ids.reshape(blocks, block)

    def step(total, pieces):
        value_piece, shell_piece, mu_piece = pieces
        mu_hot = (mu_piece[None, :] == jnp.arange(MUBINS, dtype=jnp.int32)[:, None]).astype(
            jnp.bfloat16
        )
        rows = (value_piece[:, None, :] * mu_hot[None]).reshape(3 * MUBINS, block)
        rows = jnp.concatenate([rows, mu_hot], axis=0)
        shell_hot = (shell_piece[None, :] == jnp.arange(SHELLS, dtype=jnp.int32)[:, None]).astype(
            jnp.bfloat16
        )
        return (
            total
            + lax.dot_general(
                rows, shell_hot, (((1,), (1,)), ((), ())), preferred_element_type=jnp.float32
            ),
            None,
        )

    start = jnp.zeros((4 * MUBINS, SHELLS), jnp.float32)
    total, _ = lax.scan(step, start, (value_blocks, shell_blocks, mu_blocks))
    return total


def body(fields, shells, mubins):
    depth_local, _, local_fields, planes, yrows = fields.shape
    gz_count = lax.axis_size("gz")
    plane_rows = planes * yrows
    own = fields.reshape(depth_local, 2, local_fields, plane_rows)
    cos_table, sin_table = dft_tables(NZ)
    spectra_lines = transform(
        lax.all_to_all(own, "gz", split_axis=3, concat_axis=0, tiled=True), cos_table, sin_table
    )
    twenty_spec = broadcast(spectra_lines[:, :, 0], "field", 0)
    shell_map, mu_map = (
        lax.all_to_all(
            shells.reshape(depth_local, plane_rows), "gz", split_axis=1, concat_axis=0, tiled=True
        ),
        lax.all_to_all(
            mubins.reshape(depth_local, plane_rows), "gz", split_axis=1, concat_axis=0, tiled=True
        ),
    )
    column_first = lax.axis_index("gz") * (plane_rows // gz_count)
    depth_span, column_span = shell_map.shape
    depth_index = jnp.arange(depth_span, dtype=jnp.int32)
    wave_z = jnp.where(depth_index >= NZ // 2, depth_index - NZ, depth_index).astype(jnp.float32)
    column_index = column_first + jnp.arange(column_span, dtype=jnp.int32)
    wave_x = (NZ // 4 + column_index // yrows).astype(jnp.float32)
    wave_y = (NZ // 8 + column_index % yrows).astype(jnp.float32)
    terms = monomials(
        wave_x[None, :] + jnp.zeros((depth_span, column_span), jnp.float32),
        wave_y[None, :],
        wave_z[:, None],
    )
    coef_rows = lax.dynamic_slice_in_dim(
        jnp.asarray(make_coef()), lax.axis_index("field") * local_fields, local_fields, 1
    )
    weights = jnp.einsum("mlj,jzc->mlzc", coef_rows, terms, precision=lax.Precision.HIGHEST)
    cross = (
        twenty_spec[:, 0][:, None] * spectra_lines[:, 0]
        + twenty_spec[:, 1][:, None] * spectra_lines[:, 1]
    )
    contrib = jnp.sum(weights * jnp.transpose(cross, (1, 0, 2))[None], axis=1).astype(jnp.bfloat16)
    partial_bins = bin_cells(
        contrib.reshape(3, depth_span * column_span), shell_map.reshape(-1), mu_map.reshape(-1)
    )
    count_gate = (lax.axis_index("field") == 0).astype(jnp.float32)
    partial_bins = jnp.concatenate(
        [partial_bins[: 3 * MUBINS], partial_bins[3 * MUBINS :] * count_gate], axis=0
    )
    total = lax.psum(partial_bins, ("field", "gz"))
    sums = total[: 3 * MUBINS].reshape(3, MUBINS, SHELLS)
    counts = total[3 * MUBINS :]
    return sums / jnp.maximum(counts, 1.0)[None]


def solution(mesh):
    in_specs = (P("gz", None, "field", None, None), P("gz", None, None), P("gz", None, None))
    out_specs = P()
    return jax.shard_map(body, mesh=mesh, in_specs=in_specs, out_specs=out_specs, check_vma=False)
```

profile of v0, /device:TPU:0, one launch (start us, length us, event | category | flops | bytes accessed | tf_op | source)
XLA Modules:
  0.0 1087.2 jit_solution(372042207242934170)
XLA Ops:
  6.5 16.0 %copy.25 = bf16[256,2,2,16,256]{0,2,1,4,3:T(2,128)(2,1)} copy(bf16[256,2,2,16,256]{4,3,2,1,0:T(8,128)(2,1)} %param.6) | data formatting | bytes 16777216 | tf_op args[0]
  22.6 6.4 all-to-all-start
  34.1 6.6 copy.28
  40.7 172.2 %all-to-all-done = bf16[256,2,2,4096]{0,2,1,3:T(2,128)(2,1)} async-done(((bf16[256,2,2,4096]{0,2,1,3:T(2,128)(2,1)}), bf16[256,2,2,4096]{0,2,1,3:T(2,128)(2,1)}, u32[]{:S(2)}, u32[]{:S(2)}) %all-to-all-start) | async-done | bytes 8388640 | tf_op jit(solution)/shard_map/all_to_all | solution.py:112
  217.7 11.4 %copy.26 = bf16[8,256,2,2,512]{1,0,4,3,2:T(8,128)(2,1)} copy(bf16[8,256,2,2,512]{1,3,2,4,0:T(2,128)(2,1)} %bitcast.7) | data formatting | bytes 16777216 | tf_op jit(solution)/shard_map/all_to_all | solution.py:112
  229.1 10.3 copy.34
  239.3 95.1 %fusion.25 = f32[2048,2,2,512]{3,0,2,1:T(8,128)} fusion(bf16[2,2,512,2048]{3,2,1,0:T(8,128)(2,1)} %bitcast.87), kind=kOutput, calls=%fused_computation.39 | convolution fusion | flops 17246978048 | bytes 25165824 | tf_op jit(solution)/shard_map/dot_general | solution.py:50
  334.4 78.5 %fusion.22 = f32[2048,2,2,512]{3,0,2,1:T(8,128)} fusion(bf16[2,2,512,2048]{3,2,1,0:T(8,128)(2,1)S(1)} %bitcast.88), kind=kOutput, calls=%fused_computation.37 | convolution fusion | flops 17246978048 | bytes 25165824 | tf_op jit(solution)/shard_map/dot_general | solution.py:47
  413.0 18.8 %slice_add_fusion = (f32[2048,1,2,512]{3,0,2,1:T(8,128)}, f32[2048,1,2,512]{3,0,2,1:T(8,128)}) fusion(f32[2048,2,2,512]{3,0,2,1:T(8,128)} %fusion.25, f32[2048,2,2,512]{3,0,2,1:T(8,128)} %fusion.22), kind=kLoop, calls=%fused_computation.44 | loop fusion | flops 4194304 | bytes 50331648 | tf_op jit(solution)/shard_map/add | solution.py:53
  431.8 7.8 fusion.28
  444.9 7.1 copy.29
  479.6 71.4 %all-to-all-done.2 = s32[256,8,512]{2,0,1:T(8,128)} async-done(((s32[256,8,512]{2,0,1:T(8,128)}), s32[256,8,512]{2,0,1:T(8,128)}, u32[]{:S(2)}, u32[]{:S(2)}) %all-to-all-start.2) | async-done | bytes 4194336 | tf_op jit(solution)/shard_map/all_to_all | solution.py:116
  556.0 57.2 %all-reduce.2.cloned.1.call-done = f32[2048,2,512]{2,0,1:T(8,128)} async-done(((f32[2048,2,512]{2,0,1:T(8,128)}), f32[2048,2,512]{2,0,1:T(8,128)}) %all-reduce.2.cloned.1.call-update) | async-done | bytes 8388624 | tf_op jit(solution)/shard_map/psum | solution.py:16
  617.6 9.4 fusion.30
  627.0 104.8 %multiply_reduce_fusion = bf16[3,2048,512]{2,0,1:T(4,128)(2,1)} fusion(f32[2,2048,512]{2,1,0:T(8,128)} %fusion.30, f32[7,2048,512]{2,1,0:T(8,128)} %fusion.40, f32[3,8,7]{2,0,1:T(4,128)} %constant.86.clone, s32[]{:T(128)S(6)} %select_n.62), kind=kOutput, calls=%fused_computation.17 | convolution fusion | flops 537919488 | bytes 44044292 | tf_op jit(solution)/shard_map/mlj,jzc->mlzc/dot_general | solution.py:138
  731.8 7.7 copy.42
  739.5 10.4 convert_element_type.71
  749.9 11.4 %copy.30 = bf16[32,3,32768]{2,1,0:T(4,128)(2,1)} copy(bf16[32,3,32768]{2,0,1:T(8,128)(2,1)} %bitcast.85) | data formatting | bytes 12582912
  761.3 278.0 %while.11 = (s32[]{:T(128)}, f32[32,256]{1,0:T(8,128)S(1)}, bf16[32,3,32768]{2,1,0:T(4,128)(2,1)}, s32[32,32768]{1,0:T(8,128)}, s32[32,32768]{1,0:T(8,128)}, /*index=5*/s32[]{:T(128)}, s32[]{:T(128)}) while((s32[]{:T(128)}, f32[32,256]{1,0:T(8,128)S(1)}, bf16[32,3,32768]{2,1,0:T(4,128)(2,1)}, s32[32,32768]{1,0:T(8,128)}, ...), condition=%wide.region_3.4_spmd.clone, body=%wide.region_2.3_spmd.clone.sunk | while | flops 550780928 | bytes 6160487 | solution.py:101
  773.4 5.5 fusion.84
  808.1 5.5 fusion.84
  903.6 5.5 fusion.84
  999.1 5.5 fusion.84
  1039.3 40.1 %psum.15 = f32[32,256]{1,0:T(8,128)S(1)} all-reduce(f32[32,256]{1,0:T(8,128)S(1)} %pad_maximum_fusion.1), channel_id=1, replica_groups=mesh['field'=4,'gz'=8] {'field','gz'}, use_global_device_ids=true, to_apply=%region_4.5 | all-reduce | flops 8192 | bytes 65536 | tf_op jit(solution)/shard_map/psum | solution.py:151
  (188 shorter events, 307.1 us)
Async XLA Ops:
  22.6 190.3 %all-to-all-start = ((bf16[256,2,2,4096]{0,2,1,3:T(2,128)(2,1)}), bf16[256,2,2,4096]{0,2,1,3:T(2,128)(2,1)}, u32[]{:S(2)}, u32[]{:S(2)}) async-start(bf16[256,2,2,4096]{0,2,1,3:T(2,128)(2,1)} %bitcast.83), calls=%async_computation | async-start | bytes 16777216 | tf_op jit(solution)/shard_map/all_to_all | solution.py:112
  212.9 239.1 %all-to-all-start.1 = ((s32[256,8,512]{2,0,1:T(8,128)}), s32[256,8,512]{2,0,1:T(8,128)}, u32[]{:S(2)}, u32[]{:S(2)}) async-start(s32[256,8,512]{2,0,1:T(8,128)} %copy.28), calls=%async_computation.1 | async-start | bytes 8388608 | tf_op jit(solution)/shard_map/all_to_all | solution.py:119
  217.4 395.8 %all-reduce.2.cloned.1.call-start = ((), (), s32[]{:S(2)}) async-start(), calls=%async_computation.3 | async-start | bytes 16777216 | tf_op jit(solution)/shard_map/psum | solution.py:16
  239.3 95.1 %copy-start = (bf16[256,8,8,256]{3,1,2,0:T(8,128)(2,1)S(1)}, bf16[256,8,8,256]{3,1,2,0:T(8,128)(2,1)}, u32[]{:S(2)}) copy-start(bf16[256,8,8,256]{3,1,2,0:T(8,128)(2,1)} %copy.34) | copy-start | bytes 25165828
  452.0 99.0 %all-to-all-start.2 = ((s32[256,8,512]{2,0,1:T(8,128)}), s32[256,8,512]{2,0,1:T(8,128)}, u32[]{:S(2)}, u32[]{:S(2)}) async-start(s32[256,8,512]{2,0,1:T(8,128)} %copy.29), calls=%async_computation.2 | async-start | bytes 8388608 | tf_op jit(solution)/shard_map/all_to_all | solution.py:116
Sparse Core Ops, SparseCore 0:
  439.8 173.3 all-reduce.1
where the time goes:
time: 1090 us
  matrix products  455 us (42%)
  waiting for transfers between devices  301 us (28%)
  local copies, waits for them, and re-layouts  197 us (18%)
  other arithmetic  63 us (6%)
  blocking collectives  40.1 us (4%)
  starting transfers between devices  16.1 us (1%)
  between operations  13.8 us (1%)
    dot_general x32, matrix products, step(): lax.dot_general(rows, shell_hot, (((1,), (1,)), ((), ())), preferred_elem...  176 us
    all_to_all x1, waiting for transfers between devices, body(): lax.all_to_all(own, 'gz', split_axis=3, concat_axis=0, tiled=True)  172 us
    dot_general x1, matrix products, body(): jnp.einsum('mlj,jzc->mlzc', coef_rows, terms, precision=lax.Precision.HIG...  105 us
    dot_general x1, matrix products, transform(): jnp.dot(sin_table, flat, preferred_element_type=jnp.float32)  95.1 us
    dot_general x1, matrix products, transform(): jnp.dot(cos_table, flat, preferred_element_type=jnp.float32)  78.5 us
    all_to_all x1, waiting for transfers between devices, body(): lax.all_to_all(shells.reshape(depth_local, plane_rows), 'gz', split_axis=...  71.4 us
    psum x1, waiting for transfers between devices, broadcast(): return lax.psum(kept, axis)  57.2 us
    dynamic_slice x32, local copies, waits for them, and re-layouts, bin_cells(): total, _ = lax.scan(step, start, (value_blocks, shell_blocks, mu_blocks))  55.3 us
  transfers between devices with their start and end apart: 4, of which 3 were waited for; matrix products, arithmetic and copies ran while one was open for 24% of the time, Pallas kernels for 0%

commit v1 on v0

v1 whole, which is shorter than its diff:
```python
import functools
import math

import jax
import jax.numpy as jnp
import numpy as np
from jax import lax
from jax.experimental import pallas as pl
from jax.experimental.pallas import tpu as pltpu
from jax.sharding import PartitionSpec as P

SHELLS = 256
MUBINS = 8
LANES = 128
LOW = 16
ROWS = 5
PAIRS = 8


def quarter_tables(length, zero):
    quarter, half = length // 4, length // 2
    shape = (2, quarter, half)
    parity = lax.broadcasted_iota(jnp.int32, shape, 0)
    row = lax.broadcasted_iota(jnp.int32, shape, 1) + zero
    column = lax.broadcasted_iota(jnp.int32, shape, 2)
    depth = 2 * column + parity
    unit = 2.0 * math.pi / length
    factor = 1.0 / math.sqrt(length)
    cos_part = jnp.cos((row * depth % length).astype(jnp.float32) * unit) * factor
    sin_row = jnp.where(row == 0, quarter, row)
    sin_part = jnp.sin((sin_row * depth % length).astype(jnp.float32) * unit) * factor
    alternate = (1 - 2 * (column % 2)).astype(jnp.float32) * factor
    sin_part = jnp.where((row == 0) & (parity == 0), alternate, sin_part)
    return jnp.concatenate(
        [cos_part.astype(jnp.bfloat16), sin_part.astype(jnp.bfloat16)], axis=1
    )


def round16(value):
    return value.astype(jnp.bfloat16).astype(jnp.float32)


def kernel(length, table_ref, lines_ref, keys_ref, wave_ref, out_ref, prod, vals):
    group, parity = pl.program_id(0), pl.program_id(1)
    quarter = length // 4
    half = length // 2
    right = lines_ref[0, :, 0].reshape(half, lines_ref.shape[-1])

    def product(i, carry):
        rows = pl.ds(pl.multiple_of(i * 256, 256), 256)
        prod[group, parity, rows, :] = jnp.dot(
            table_ref[0, rows, :], right, preferred_element_type=jnp.float32
        )
        return carry

    lax.fori_loop(0, half // 256, product, 0)

    @pl.when((group == pl.num_programs(0) - 1) & (parity == 1))
    def _():
        groups, local = prod.shape[0], prod.shape[3] // (2 * LANES)
        fields = groups * local
        out_ref[...] = jnp.zeros_like(out_ref)
        wave_x = wave_ref[0:1, :]
        wave_y = wave_ref[1:2, :]
        low_iota = lax.broadcasted_iota(jnp.int32, (16, LANES), 0).astype(jnp.float32)
        iotas = [(low_iota + 16.0 * j).astype(jnp.bfloat16) for j in range(LANES // 16)]
        one = jnp.ones((16, LANES), jnp.bfloat16)
        none = jnp.zeros((16, LANES), jnp.bfloat16)

        def tile(t, carry):
            first = pl.multiple_of(t * 8, 8)
            row = lax.broadcasted_iota(jnp.int32, (8, LANES), 0) + first
            special = row == 0

            def load(a, c, parity, sine):
                g, i = a // local, a % local
                at = (c * local + i) * LANES
                return prod[g, parity, pl.ds(sine * quarter + first, 8), at : at + LANES]

            def spectra(a):
                parts = []
                for c in range(2):
                    ec, oc = load(a, c, 0, 0), load(a, c, 1, 0)
                    es, os = load(a, c, 0, 1), load(a, c, 1, 1)
                    p, q, m, n = ec + oc, es + os, ec - oc, os - es
                    parts.append(
                        (
                            (p, jnp.where(special, 0.0, q)),
                            (m, jnp.where(special, 0.0, n)),
                            (jnp.where(special, es, m), jnp.where(special, os, -n)),
                            (jnp.where(special, es, p), jnp.where(special, -os, -q)),
                        )
                    )
                u, v = parts
                return [(u[j][0] + v[j][1], v[j][0] - u[j][1]) for j in range(4)]

            k = row.astype(jnp.float32)
            zero_wave = (0.0, -half, quarter, -quarter)
            waves = (k, half - k, k - half, -k)
            base = spectra(0)
            second = None
            totals = [None] * 4
            saved = [None] * 4
            pending = [None] * 4
            for a in range(fields):
                spec = base if a == 0 else spectra(a)
                for j in range(4):
                    cross = base[j][0] * spec[j][0] + base[j][1] * spec[j][1]
                    if a == 0:
                        wz = jnp.where(special, float(zero_wave[j]), waves[j])
                        square = wave_x * wave_x + wave_y * wave_y + wz * wz
                        saved[j] = (wz, 1.0 / square)
                        vals[0, j * 8 : j * 8 + 8] = round16(cross)
                        continue
                    wz, inverse = saved[j]
                    if a == 1:
                        vals[1, j * 8 : j * 8 + 8] = round16(cross)
                        term = -0.5 * cross
                    else:
                        weight = (
                            1.5 * wave_x * wave_x,
                            1.5 * wave_y * wave_y,
                            1.5 * wz * wz,
                            3.0 * wave_x * wave_y,
                            3.0 * wave_x * wz,
                            3.0 * wave_y * wz,
                        )[a - 2]
                        term = weight * inverse * cross
                    pending[j] = term if pending[j] is None else pending[j] + term
                    if a % local == local - 1:
                        rounded = round16(pending[j])
                        totals[j] = rounded if totals[j] is None else totals[j] + rounded
                        pending[j] = None
            for j in range(4):
                high = round16(totals[j])
                vals[2, j * 8 : j * 8 + 8] = high
                vals[3, j * 8 : j * 8 + 8] = totals[j] - high
                key = keys_ref[j, pl.ds(first, 8), :]
                upper = key // LOW
                vals[4, j * 8 : j * 8 + 8] = (key - upper * LOW).astype(jnp.float32)
                vals[5, j * 8 : j * 8 + 8] = upper.astype(jnp.float32)
            total = out_ref[...]
            for start in range(0, 32, PAIRS):
                left, hot = [], []
                for r in range(start, start + PAIRS):
                    spread = [
                        jnp.broadcast_to(vals[i, r : r + 1], (16, LANES)).astype(jnp.bfloat16)
                        for i in range(6)
                    ]
                    match = spread[4] == iotas[0]
                    left.append(
                        jnp.concatenate(
                            [jnp.where(match, spread[i], none) for i in range(4)]
                            + [jnp.where(match, one, none)],
                            axis=0,
                        )
                    )
                    hot.append(
                        jnp.concatenate(
                            [jnp.where(spread[5] == it, one, none) for it in iotas], axis=0
                        )
                    )
                total = total + lax.dot_general(
                    jnp.concatenate(left, axis=1),
                    jnp.concatenate(hot, axis=1),
                    (((1,), (1,)), ((), ())),
                    preferred_element_type=jnp.float32,
                )
            out_ref[...] = total
            return carry

        lax.fori_loop(0, quarter // 8, tile, 0)


def body(fields, shells, mubins):
    depth_local, _, local_fields, planes, yrows = fields.shape
    gz_count, field_count = lax.axis_size("gz"), lax.axis_size("field")
    devices = gz_count * field_count
    length = depth_local * gz_count
    half, quarter = length // 2, length // 4
    plane_rows = planes * yrows
    width = plane_rows // devices
    me_gz, me_field = lax.axis_index("gz"), lax.axis_index("field")

    share = plane_rows // field_count
    packed = shells + mubins * 65536
    packed = lax.dynamic_slice_in_dim(
        packed.reshape(depth_local, plane_rows), me_field * share, share, 1
    )
    packed = packed.reshape(depth_local, gz_count, width).transpose(1, 0, 2)
    packed = lax.all_to_all(packed, "gz", split_axis=0, concat_axis=0, tiled=True)
    packed = packed.reshape(length, width)
    keys = (packed & 65535) * MUBINS + packed // 65536
    if width < LANES:
        keys = jnp.pad(keys, ((0, 0), (0, LANES - width)), constant_values=SHELLS * MUBINS)
    keys = jnp.stack(
        [
            keys[:quarter],
            jnp.flip(keys[quarter + 1 : half + 1], 0),
            jnp.concatenate([keys[quarter : quarter + 1], keys[half + 1 : half + quarter]], 0),
            jnp.concatenate(
                [keys[half + quarter : half + quarter + 1], jnp.flip(keys[half + quarter + 1 :], 0)],
                0,
            ),
        ]
    )

    lines = fields.reshape(depth_local // 2, 2, 2, local_fields, devices, width)
    lines = lines.transpose(4, 1, 0, 2, 3, 5).reshape(
        devices, 2, depth_local // 2, 2 * local_fields * width
    )
    lines = lax.all_to_all(lines, ("field", "gz"), split_axis=0, concat_axis=0, tiled=True)
    lines = lines.reshape(field_count, gz_count, 2, depth_local // 2, 2 * local_fields, width)
    if width < LANES:
        lines = jnp.pad(lines, ((0, 0),) * 5 + ((0, LANES - width),))
    span = 2 * local_fields * LANES
    lines = lines.reshape(field_count, gz_count, 2, depth_local // 2, span)

    table = quarter_tables(length, jnp.minimum(me_gz, 0))
    column = (me_field * gz_count + me_gz) * width + jnp.arange(LANES, dtype=jnp.int32)
    waves = jnp.stack([length // 4 + column // yrows, length // 8 + column % yrows])
    waves = jnp.pad(waves.astype(jnp.float32), ((0, 6), (0, 0)))

    total = pl.pallas_call(
        functools.partial(kernel, length),
        grid=(field_count, 2),
        out_shape=jax.ShapeDtypeStruct((ROWS * LOW, LANES), jnp.float32),
        in_specs=[
            pl.BlockSpec((1, half, half), lambda f, p: (p, 0, 0)),
            pl.BlockSpec(
                (1, gz_count, 1, depth_local // 2, span), lambda f, p: (f, 0, p, 0, 0)
            ),
            pl.BlockSpec((4, quarter, LANES), lambda f, p: (0, 0, 0)),
            pl.BlockSpec((8, LANES), lambda f, p: (0, 0)),
        ],
        out_specs=pl.BlockSpec((ROWS * LOW, LANES), lambda f, p: (0, 0)),
        scratch_shapes=[
            pltpu.VMEM((field_count, 2, half, span), jnp.float32),
            pltpu.VMEM((6, 32, LANES), jnp.float32),
        ],
        compiler_params=pltpu.CompilerParams(vmem_limit_bytes=48 * 1024 * 1024),
    )(table, lines, keys, waves)

    total = lax.psum(total, ("field", "gz"))
    total = total.reshape(ROWS, 2, MUBINS, LANES).transpose(0, 2, 3, 1)
    total = total.reshape(ROWS, MUBINS, SHELLS)
    sums = jnp.stack([total[0], total[1], total[2] + total[3]])
    return sums / jnp.maximum(total[4], 1.0)[None]


def solution(mesh):
    in_specs = (P("gz", None, "field", None, None), P("gz", None, None), P("gz", None, None))
    return jax.shard_map(body, mesh=mesh, in_specs=in_specs, out_specs=P(), check_vma=False)
```

time: 1090 us -> 346 us (0.32)
  matrix products: 455 us -> 0 us
  waiting for transfers between devices: 301 us -> 147 us
  local copies, waits for them, and re-layouts: 197 us -> 50.7 us
  Pallas kernels: 0 us -> 46.8 us
  other arithmetic: 63 us -> 43.4 us
  between operations: 13.8 us -> 0.19 us
    dot_general x35 -> x0, matrix products: 455 us -> none  [the longest x32 176 us: step(): lax.dot_general(rows, shell_hot, (((1,), (1,)), ((), ())), preferred_elem...]
    all_to_all x3 -> x2, waiting for transfers between devices: 244 us -> 147 us  [the longest x1 147 us: body(): lax.all_to_all(lines, ('field', 'gz'), split_axis=0, concat_axis=0, tiled...]
    psum x1 -> x0, waiting for transfers between devices: 57.2 us -> none  [broadcast(): return lax.psum(kept, axis)]
    dynamic_slice x32 -> x1, local copies, waits for them, and re-layouts: 55.3 us -> 2.28 us  [body(): lax.dynamic_slice_in_dim(packed.reshape(depth_local, plane_rows), me_fiel...]
    pallas_call x0 -> x1, Pallas kernels: none -> 46.8 us  [body(): pl.pallas_call(functools.partial(kernel, length), grid=(field_count, 2),...]
    unnamed x6 -> x2, local copies, waits for them, and re-layouts: 40.2 us -> 2.19 us
    mul x33 -> x0, local copies, waits for them, and re-layouts: 38 us -> none  [the longest x32 33.5 us: step(): rows = (value_piece[:, None, :] * mu_hot[None]).reshape(3 * MUBINS, block)]
    all_to_all x5 -> x1, local copies, waits for them, and re-layouts: 35.5 us -> 0.32 us  [body(): lax.all_to_all(packed, 'gz', split_axis=0, concat_axis=0, tiled=True)]
  transfers between devices with their start and end apart: 4 -> 2, of which waited for: 3 -> 1; matrix products, arithmetic and copies ran while one was open for 24% -> 22% of each run, Pallas kernels for 0% -> 0%
where the time goes in v1:
time: 346 us; the launch traced here: 345 us
  waiting for transfers between devices  147 us (42%)
  local copies, waits for them, and re-layouts  50.7 us (15%)
  Pallas kernels  46.8 us (14%)
  blocking collectives  44.2 us (13%)
  other arithmetic  43.4 us (13%)
  starting transfers between devices  12.7 us (4%)
    all_to_all x1, waiting for transfers between devices, body(): lax.all_to_all(lines, ('field', 'gz'), split_axis=0, concat_axis=0, tiled...  147 us
    pallas_call x1, Pallas kernels, body(): pl.pallas_call(functools.partial(kernel, length), grid=(field_count, 2),...  46.8 us
    psum x1, blocking collectives, body(): total = lax.psum(total, ('field', 'gz'))  44.2 us
    convert_element_type x1, other arithmetic, quarter_tables(): cos_part.astype(jnp.bfloat16)  32.9 us
    transpose x1, local copies, waits for them, and re-layouts, body(): lines.transpose(4, 1, 0, 2, 3, 5)  13.4 us
    reshape x1, local copies, waits for them, and re-layouts, body(): lines.transpose(4, 1, 0, 2, 3, 5)  13.2 us
    reshape x1, local copies, waits for them, and re-layouts, body(): lines = fields.reshape(depth_local // 2, 2, 2, local_fields, devices, width)  13 us
  transfers between devices with their start and end apart: 2, of which 1 were waited for; matrix products, arithmetic and copies ran while one was open for 22% of the time, Pallas kernels for 0%

profile of v1, /device:TPU:0, one launch (start us, length us, event | category | flops | bytes accessed | tf_op | source)
XLA Modules:
  0.0 345.4 jit_solution(12974924667103318226)
XLA Ops:
  0.0 6.5 %multiply_add_fusion = s32[256,16,256]{2,1,0:T(8,128)} fusion(s32[256,16,256]{2,1,0:T(8,128)} %param.4, s32[256,16,256]{2,1,0:T(8,128)} %param.5), kind=kLoop, calls=%fused_computation.20 | loop fusion | flops 2097152 | bytes 12582912 | tf_op jit(solution)/shard_map/add | solution.py:186
  6.5 5.3 %copy.14 = s32[256,16,256]{0,2,1:T(8,128)} copy(s32[256,16,256]{2,1,0:T(8,128)} %multiply_add_fusion) | data formatting | bytes 8388608 | tf_op jit(solution)/shard_map/add | solution.py:186
  11.7 2.3 constant_dynamic-slice_fusion
  14.0 6.4 %all-to-all-start.1 = ((s32[8,256,128]{1,2,0:T(8,128)}), s32[8,256,128]{1,2,0:T(8,128)S(1)}, u32[]{:S(2)}, u32[]{:S(2)}) async-start(s32[8,256,128]{1,2,0:T(8,128)} %bitcast.4), calls=%async_computation.1 | async-start | bytes 2097152 | tf_op jit(solution)/shard_map/all_to_all | solution.py:191
  20.4 13.0 %reshape.130 = bf16[128,2,2,2,32,128]{5,4,3,2,1,0:T(8,128)(2,1)} reshape(bf16[256,2,2,16,256]{4,3,2,1,0:T(8,128)(2,1)} %param.3) | data formatting | bytes 16777216 | tf_op jit(solution)/shard_map/reshape | solution.py:208
  33.3 13.4 %copy.13 = bf16[32,2,128,2,2,128]{5,4,3,2,1,0:T(2,128)(2,1)} copy(bf16[32,2,128,2,2,128]{5,0,4,3,1,2:T(8,128)(2,1)} %bitcast.43) | data formatting | bytes 16777216 | tf_op jit(solution)/shard_map/transpose | solution.py:209
  46.7 13.2 %reshape.131 = bf16[32,2,128,512]{3,2,1,0:T(8,128)(2,1)} reshape(bf16[32,2,128,2,2,128]{5,4,3,2,1,0:T(2,128)(2,1)} %copy.13) | data formatting | bytes 16777216 | tf_op jit(solution)/shard_map/reshape | solution.py:209
  59.9 6.4 %all-to-all-start = ((bf16[32,2,128,512]{3,2,1,0:T(8,128)(2,1)}), bf16[32,2,128,512]{3,2,1,0:T(8,128)(2,1)}, u32[]{:S(2)}, u32[]{:S(2)}) async-start(bf16[32,2,128,512]{3,2,1,0:T(8,128)(2,1)} %reshape.131), calls=%async_computation | async-start | bytes 16777216 | tf_op jit(solution)/shard_map/all_to_all | solution.py:212
  66.4 32.9 %fusion.5 = (bf16[2,512,1024]{2,1,0:T(8,128)(2,1)S(1)}, bf16[2,512,1024]{2,1,0:T(8,128)(2,1)S(1)}) fusion(s32[1024]{0:T(1024)S(1)} %iota_multiply_fusion, s32[512]{0:T(512)S(1)} %iota_add_fusion.1, s32[1024]{0:T(1024)S(1)} %get-tuple-element.17, s32[1024]{0:T(1024)S(1)} %get-tuple-element.18, pred[1024]{0:T(1024)(128)(4,1)S(1)} %fusion.21, ...), kind=kLoop, calls=%fused_computation.11 | loop fusion | flops 42991616 | bytes 4210178 | tf_op jit(solution)/shard_map/convert_element_type | solution.py:35
  99.3 2.4 pad_maximum_fusion.table_ref
  101.7 0.3 copy.15
  102.0 0.7 fusion.14
  102.8 0.3 rev.9
  103.2 0.1 rev.8
  103.4 0.1 pad_add_fusion.keys_ref
  103.4 147.4 %all-to-all-done = bf16[32,2,128,512]{3,2,1,0:T(8,128)(2,1)} async-done(((bf16[32,2,128,512]{3,2,1,0:T(8,128)(2,1)}), bf16[32,2,128,512]{3,2,1,0:T(8,128)(2,1)}, u32[]{:S(2)}, u32[]{:S(2)}) %all-to-all-start) | async-done | bytes 8388640 | tf_op jit(solution)/shard_map/all_to_all | solution.py:212
  250.9 2.2 copy-done
  253.1 46.8 %shard_map.37 = f32[80,128]{1,0:T(8,128)S(1)} custom-call(bf16[2,1024,1024]{2,1,0:T(8,128)(2,1)S(1)} %copy-done, bf16[4,8,2,128,512]{4,3,2,1,0:T(8,128)(2,1)} %bitcast.1.lines_ref, s32[4,512,128]{2,1,0:T(8,128)S(1)} %pad_add_fusion.keys_ref, f32[8,128]{1,0:T(8,128)S(1)} %pad.4.wave_ref), custom_call_target="tpu_custom_call" | custom-call | tf_op jit(solution)/shard_map/pallas_call | solution.py:224
  299.9 0.3 copy.16
  300.2 44.2 %psum.7 = f32[5,8,128,2]{1,3,2,0:T(2,128)S(1)} all-reduce(f32[5,8,128,2]{1,3,2,0:T(2,128)S(1)} %bitcast.45), channel_id=1, replica_groups=mesh['field'=4,'gz'=8] {'field','gz'}, use_global_device_ids=true, to_apply=%region_0.1 | all-reduce | flops 10240 | bytes 81920 | tf_op jit(solution)/shard_map/psum | solution.py:244
  344.3 0.1 slice_maximum_fusion
  344.6 0.1 copy.17
  344.7 0.1 copy.20
  344.8 0.6 maximum_divide_fusion
  (17 shorter events, 0.3 us)
Async XLA Ops:
  14.0 45.9 %all-to-all-start.1 = ((s32[8,256,128]{1,2,0:T(8,128)}), s32[8,256,128]{1,2,0:T(8,128)S(1)}, u32[]{:S(2)}, u32[]{:S(2)}) async-start(s32[8,256,128]{1,2,0:T(8,128)} %bitcast.4), calls=%async_computation.1 | async-start | bytes 2097152 | tf_op jit(solution)/shard_map/all_to_all | solution.py:191
  59.9 191.0 %all-to-all-start = ((bf16[32,2,128,512]{3,2,1,0:T(8,128)(2,1)}), bf16[32,2,128,512]{3,2,1,0:T(8,128)(2,1)}, u32[]{:S(2)}, u32[]{:S(2)}) async-start(bf16[32,2,128,512]{3,2,1,0:T(8,128)(2,1)} %reshape.131), calls=%async_computation | async-start | bytes 16777216 | tf_op jit(solution)/shard_map/all_to_all | solution.py:212
  250.9 2.2 copy-start

commit v2 on v1

--- a/solution.py
+++ b/solution.py
@@ -172,6 +172,126 @@
         lax.fori_loop(0, quarter // 8, tile, 0)
 
 
+def relayout_kernel(fields_ref, out_ref):
+    for c in range(2):
+        for i in range(fields_ref.shape[2]):
+            at = (c * fields_ref.shape[2] + i) * LANES
+            for h in range(out_ref.shape[1]):
+                block = fields_ref[:, c, i, :, h * LANES : (h + 1) * LANES]
+                block = block.reshape(16, 2, block.shape[1], LANES)
+                for parity in range(2):
+                    out_ref[:, h, parity, :, at : at + LANES] = jnp.swapaxes(
+                        block[:, parity], 0, 1
+                    )
+
+
+def relayout(fields):
+    depth, _, local, planes, yrows = fields.shape
+    parts = yrows // LANES
+    out = pl.pallas_call(
+        relayout_kernel,
+        grid=(depth // 32,),
+        out_shape=jax.ShapeDtypeStruct(
+            (planes, parts, 2, depth // 2, 2 * local * LANES), fields.dtype
+        ),
+        in_specs=[pl.BlockSpec((32, 2, local, planes, yrows), lambda i: (i, 0, 0, 0, 0))],
+        out_specs=pl.BlockSpec(
+            (planes, parts, 2, 16, 2 * local * LANES), lambda i: (0, 0, 0, i, 0)
+        ),
+    )(fields)
+    return out.reshape(planes * parts, 2, depth // 2, 2 * local * LANES)
+
+
+def reduce_kernel(field_count, gz_count, mine_ref, out_ref, parts, answer, send, recv, send2, recv2):
+    devices = field_count * gz_count
+    me_field, me_gz = lax.axis_index("field"), lax.axis_index("gz")
+    me = me_field * gz_count + me_gz
+
+    def peer(step):
+        other = lax.rem(me + step, devices)
+        return other, (other // gz_count, lax.rem(other, gz_count))
+
+    barrier = pltpu.get_barrier_semaphore()
+
+    def greet(step, carry):
+        _, place = peer(step)
+        pl.semaphore_signal(
+            barrier, inc=1, device_id=place, device_id_type=pl.DeviceIdType.MESH
+        )
+        return carry
+
+    lax.fori_loop(1, devices, greet, 0)
+    pl.semaphore_wait(barrier, devices - 1)
+
+    def scatter(step):
+        other, place = peer(step)
+        return pltpu.make_async_remote_copy(
+            src_ref=mine_ref.at[other],
+            dst_ref=parts.at[step],
+            send_sem=send.at[step],
+            recv_sem=recv.at[step],
+            device_id=place,
+            device_id_type=pl.DeviceIdType.MESH,
+        )
+
+    def gather(step):
+        _, place = peer(step)
+        return pltpu.make_async_remote_copy(
+            src_ref=answer,
+            dst_ref=out_ref.at[me],
+            send_sem=send2.at[step],
+            recv_sem=recv2.at[step],
+            device_id=place,
+            device_id_type=pl.DeviceIdType.MESH,
+        )
+
+    def start(copy):
+        def run(step, carry):
+            copy(step).start()
+            return carry
+
+        lax.fori_loop(1, devices, run, 0)
+
+    start(scatter)
+
+    def collect(step, total):
+        scatter(step).wait_recv()
+        return total + parts[step]
+
+    answer[...] = lax.fori_loop(1, devices, collect, mine_ref[me])
+    start(gather)
+    out_ref[me] = answer[...]
+
+    def finish(step, carry):
+        scatter(step).wait_send()
+        gather(step).wait()
+        return carry
+
+    lax.fori_loop(1, devices, finish, 0)
+
+
+def all_reduce(total, field_count, gz_count):
+    devices = field_count * gz_count
+    rows = max(1, total.shape[0] // devices)
+    total = jnp.pad(total, ((0, devices * rows - total.shape[0]), (0, 0)))
+    total = total.reshape(devices, rows, LANES)
+    return pl.pallas_call(
+        functools.partial(reduce_kernel, field_count, gz_count),
+        out_shape=jax.ShapeDtypeStruct(total.shape, jnp.float32),
+        in_specs=[pl.BlockSpec(memory_space=pltpu.VMEM)],
+        out_specs=pl.BlockSpec(memory_space=pltpu.VMEM),
+        scratch_shapes=[
+            pltpu.VMEM(total.shape, jnp.float32),
+            pltpu.VMEM(total.shape[1:], jnp.float32),
+            pltpu.SemaphoreType.DMA((devices,)),
+            pltpu.SemaphoreType.DMA((devices,)),
+            pltpu.SemaphoreType.DMA((devices,)),
+            pltpu.SemaphoreType.DMA((devices,)),
+        ],
+        compiler_params=pltpu.CompilerParams(collective_id=0, has_side_effects=True),
+    )(total).reshape(devices * rows, LANES)
+
+
 def body(fields, shells, mubins):
     depth_local, _, local_fields, planes, yrows = fields.shape
     gz_count, field_count = lax.axis_size("gz"), lax.axis_size("field")
@@ -181,6 +301,15 @@
     plane_rows = planes * yrows
     width = plane_rows // devices
     me_gz, me_field = lax.axis_index("gz"), lax.axis_index("field")
+
+    if width == LANES and depth_local % 32 == 0:
+        lines = relayout(fields)
+    else:
+        lines = fields.reshape(depth_local // 2, 2, 2, local_fields, devices, width)
+        lines = lines.transpose(4, 1, 0, 2, 3, 5).reshape(
+            devices, 2, depth_local // 2, 2 * local_fields * width
+        )
+    lines, shells, mubins = lax.optimization_barrier((lines, shells, mubins))
 
     share = plane_rows // field_count
     packed = shells + mubins * 65536
@@ -205,10 +334,6 @@
         ]
     )
 
-    lines = fields.reshape(depth_local // 2, 2, 2, local_fields, devices, width)
-    lines = lines.transpose(4, 1, 0, 2, 3, 5).reshape(
-        devices, 2, depth_local // 2, 2 * local_fields * width
-    )
     lines = lax.all_to_all(lines, ("field", "gz"), split_axis=0, concat_axis=0, tiled=True)
     lines = lines.reshape(field_count, gz_count, 2, depth_local // 2, 2 * local_fields, width)
     if width < LANES:
@@ -241,11 +366,12 @@
         compiler_params=pltpu.CompilerParams(vmem_limit_bytes=48 * 1024 * 1024),
     )(table, lines, keys, waves)
 
-    total = lax.psum(total, ("field", "gz"))
-    total = total.reshape(ROWS, 2, MUBINS, LANES).transpose(0, 2, 3, 1)
-    total = total.reshape(ROWS, MUBINS, SHELLS)
-    sums = jnp.stack([total[0], total[1], total[2] + total[3]])
-    return sums / jnp.maximum(total[4], 1.0)[None]
+    total = total.reshape(ROWS, LOW, LANES)
+    total = jnp.concatenate([total[:2], total[2:3] + total[3:4], total[4:]])
+    total = all_reduce(total.reshape(-1, LANES), field_count, gz_count)[: 4 * LOW]
+    total = total.reshape(4, 2, MUBINS, LANES).transpose(0, 2, 3, 1)
+    total = total.reshape(4, MUBINS, SHELLS)
+    return total[:3] / jnp.maximum(total[3], 1.0)[None]
 
 
 def solution(mesh):

time: 346 us -> 310 us (0.90)
  local copies, waits for them, and re-layouts: 50.7 us -> 11.4 us
  Pallas kernels: 46.8 us -> 70.6 us
  blocking collectives: 44.2 us -> 32.7 us
  starting transfers between devices: 12.7 us -> 3.91 us
    psum x1 -> x0, blocking collectives: 44.2 us -> none  [body(): total = lax.psum(total, ('field', 'gz'))]
    all_to_all x0 -> x1, blocking collectives: none -> 32.7 us  [body(): lax.all_to_all(packed, 'gz', split_axis=0, concat_axis=0, tiled=True)]
    reshape x3 -> x0, local copies, waits for them, and re-layouts: 26.4 us -> none  [the longest x1 13.2 us: body(): lines.transpose(4, 1, 0, 2, 3, 5)]
    pallas_call x0 -> x2, Pallas kernels: none -> 23.4 us  [the longest x1 13.5 us: all_reduce(): pl.pallas_call(functools.partial(reduce_kernel, field_count, gz_count), o...]
    transpose x1 -> x0, local copies, waits for them, and re-layouts: 13.4 us -> none  [body(): lines.transpose(4, 1, 0, 2, 3, 5)]
    all_to_all x1 -> x0, starting transfers between devices: 6.35 us -> none  [body(): lax.all_to_all(packed, 'gz', split_axis=0, concat_axis=0, tiled=True)]
  transfers between devices with their start and end apart: 2 -> 1, of which waited for: 1 -> 1; matrix products, arithmetic and copies ran while one was open for 22% -> 12% of each run, Pallas kernels for 0% -> 0%
where the time goes in v2:
time: 310 us
  waiting for transfers between devices  147 us (47%)
  Pallas kernels  70.6 us (23%)
  other arithmetic  43.3 us (14%)
  blocking collectives  32.7 us (11%)
  local copies, waits for them, and re-layouts  11.4 us (4%)
  starting transfers between devices  3.91 us (1%)
    all_to_all x1, waiting for transfers between devices, body(): lax.all_to_all(lines, ('field', 'gz'), split_axis=0, concat_axis=0, tiled...  147 us
    pallas_call x1, Pallas kernels, body(): pl.pallas_call(functools.partial(kernel, length), grid=(field_count, 2),...  47.2 us
    convert_element_type x1, other arithmetic, quarter_tables(): cos_part.astype(jnp.bfloat16)  32.9 us
    all_to_all x1, blocking collectives, body(): lax.all_to_all(packed, 'gz', split_axis=0, concat_axis=0, tiled=True)  32.7 us
    pallas_call x1, Pallas kernels, all_reduce(): pl.pallas_call(functools.partial(reduce_kernel, field_count, gz_count), o...  13.5 us
    pallas_call x1, Pallas kernels, relayout(): pl.pallas_call(relayout_kernel, grid=(depth // 32,), out_shape=jax.ShapeD...  9.86 us
    add x1, other arithmetic, body(): packed = shells + mubins * 65536  6.46 us
  transfers between devices with their start and end apart: 1, of which 1 were waited for; matrix products, arithmetic and copies ran while one was open for 12% of the time, Pallas kernels for 0%

profile of v2, /device:TPU:0, one launch (start us, length us, event | category | flops | bytes accessed | tf_op | source)
XLA Modules:
  0.0 309.6 jit_solution(2226860830711925299)
XLA Ops:
  0.0 9.9 %shard_map.37 = bf16[16,2,2,128,512]{4,3,2,1,0:T(8,128)(2,1)} custom-call(bf16[256,2,2,16,256]{4,3,2,1,0:T(8,128)(2,1)} %fields_ref.1), custom_call_target="tpu_custom_call" | custom-call | tf_op jit(solution)/shard_map/pallas_call | solution.py:191
  9.9 6.5 %multiply_add_fusion = s32[256,16,256]{2,1,0:T(8,128)} fusion(s32[256,16,256]{2,1,0:T(8,128)} %param.4, s32[256,16,256]{2,1,0:T(8,128)} %param.5), kind=kLoop, calls=%fused_computation.20 | loop fusion | flops 2097152 | bytes 12582912 | tf_op jit(solution)/shard_map/add | solution.py:315
  16.3 5.3 %copy.5 = s32[256,16,256]{0,2,1:T(8,128)} copy(s32[256,16,256]{2,1,0:T(8,128)} %multiply_add_fusion) | data formatting | bytes 8388608 | tf_op jit(solution)/shard_map/add | solution.py:315
  21.6 1.3 constant_dynamic-slice_fusion
  22.9 32.7 %all_to_all.10 = s32[8,256,128]{1,2,0:T(8,128)S(1)} all-to-all(s32[8,256,128]{1,2,0:T(8,128)S(1)} %bitcast.46), channel_id=1, replica_groups=mesh['field'=4,'gz'=8] {'gz'}, dimensions={0} | all-to-all | bytes 2097152 | tf_op jit(solution)/shard_map/all_to_all | solution.py:320
  55.6 3.9 %all-to-all-start = ((bf16[32,2,128,512]{3,2,1,0:T(8,128)(2,1)}), bf16[32,2,128,512]{3,2,1,0:T(8,128)(2,1)}, u32[]{:S(2)}, u32[]{:S(2)}) async-start(bf16[32,2,128,512]{3,2,1,0:T(8,128)(2,1)} %bitcast.44), calls=%async_computation | async-start | bytes 16777216 | tf_op jit(solution)/shard_map/all_to_all | solution.py:337
  59.6 32.9 %fusion.5 = (bf16[2,512,1024]{2,1,0:T(8,128)(2,1)S(1)}, bf16[2,512,1024]{2,1,0:T(8,128)(2,1)S(1)}) fusion(s32[1024]{0:T(1024)S(1)} %iota_multiply_fusion, s32[512]{0:T(512)S(1)} %iota_add_fusion.1, s32[1024]{0:T(1024)S(1)} %get-tuple-element.21, s32[1024]{0:T(1024)S(1)} %get-tuple-element.22, pred[1024]{0:T(1024)(128)(4,1)S(1)} %fusion.22, ...), kind=kLoop, calls=%fused_computation.11 | loop fusion | flops 42991616 | bytes 4210178 | tf_op jit(solution)/shard_map/convert_element_type | solution.py:35
  92.5 2.4 pad_maximum_fusion.table_ref
  94.9 0.3 copy.6
  95.3 0.7 fusion.14
  96.0 0.3 rev.9
  96.4 0.1 rev.8
  96.6 0.1 pad_add_fusion.keys_ref
  96.7 147.4 %all-to-all-done = bf16[32,2,128,512]{3,2,1,0:T(8,128)(2,1)} async-done(((bf16[32,2,128,512]{3,2,1,0:T(8,128)(2,1)}), bf16[32,2,128,512]{3,2,1,0:T(8,128)(2,1)}, u32[]{:S(2)}, u32[]{:S(2)}) %all-to-all-start) | async-done | bytes 8388640 | tf_op jit(solution)/shard_map/all_to_all | solution.py:337
  244.1 0.0 copy-start
  244.1 2.2 copy-done
  246.3 47.2 %shard_map.38 = f32[80,128]{1,0:T(8,128)S(1)} custom-call(bf16[2,1024,1024]{2,1,0:T(8,128)(2,1)S(1)} %copy-done, bf16[4,8,2,128,512]{4,3,2,1,0:T(8,128)(2,1)} %bitcast.1.lines_ref, s32[4,512,128]{2,1,0:T(8,128)S(1)} %pad_add_fusion.keys_ref, f32[8,128]{1,0:T(8,128)S(1)} %pad.4.wave_ref), custom_call_target="tpu_custom_call" | custom-call | tf_op jit(solution)/shard_map/pallas_call | solution.py:349
  293.6 0.6 pad_maximum_fusion.1
  294.2 13.5 %shard_map.39 = f32[32,2,128]{2,1,0:T(2,128)} custom-call(f32[32,2,128]{2,1,0:T(2,128)} %bitcast.53), custom_call_target="tpu_custom_call" | custom-call | tf_op jit(solution)/shard_map/pallas_call | solution.py:278
  307.7 1.0 copy.7
  308.8 0.1 slice_maximum_fusion
  308.9 0.7 copy.8
  (17 shorter events, 0.2 us)
Async XLA Ops:
  55.6 188.5 %all-to-all-start = ((bf16[32,2,128,512]{3,2,1,0:T(8,128)(2,1)}), bf16[32,2,128,512]{3,2,1,0:T(8,128)(2,1)}, u32[]{:S(2)}, u32[]{:S(2)}) async-start(bf16[32,2,128,512]{3,2,1,0:T(8,128)(2,1)} %bitcast.44), calls=%async_computation | async-start | bytes 16777216 | tf_op jit(solution)/shard_map/all_to_all | solution.py:337
  244.1 2.2 copy-start

commit v3 on v2

v3 whole, which is shorter than its diff:
```python
import functools
import math

import jax
import jax.numpy as jnp
import numpy as np
from jax import lax
from jax.experimental import pallas as pl
from jax.experimental.pallas import tpu as pltpu
from jax.sharding import PartitionSpec as P

SHELLS = 256
MUBINS = 8
LANES = 128
LOW = 16
ROWS = 5
PAIRS = 8


def quarter_tables(length, zero):
    quarter, half = length // 4, length // 2
    unit = 2.0 * math.pi / length
    factor = 1.0 / math.sqrt(length)

    def pair(rows, stride):
        shape = (2, rows, half)
        parity = lax.broadcasted_iota(jnp.int32, shape, 0)
        row = lax.broadcasted_iota(jnp.int32, shape, 1) * stride + zero
        depth = 2 * lax.broadcasted_iota(jnp.int32, shape, 2) + parity
        angle = (row * depth % length).astype(jnp.float32) * unit
        return jnp.cos(angle), jnp.sin(angle)

    fine = 16
    ca, sa, cb, sb = lax.optimization_barrier(pair(quarter // fine, fine) + pair(fine, 1))
    ca, sa, cb, sb = ca[:, :, None], sa[:, :, None], cb[:, None], sb[:, None]
    cos_part = ((ca * cb - sa * sb) * factor).reshape(2, quarter, half)
    sin_part = ((sa * cb + ca * sb) * factor).reshape(2, quarter, half)
    row = lax.broadcasted_iota(jnp.int32, sin_part.shape, 1)
    column = lax.broadcasted_iota(jnp.int32, sin_part.shape, 2)
    alternate = (1 - 2 * (column % 2)).astype(jnp.float32) * factor
    sin_part = jnp.where(row == 0, alternate, sin_part)
    return jnp.concatenate(
        [cos_part.astype(jnp.bfloat16), sin_part.astype(jnp.bfloat16)], axis=1
    )


def round16(value):
    return value.astype(jnp.bfloat16).astype(jnp.float32)


def unpack(index_ref, keys):
    depth = index_ref.shape[1]

    def block(g, carry):
        word = index_ref[g]
        mu = word // 65536
        key = (word - mu * 65536) * MUBINS + mu
        upper = key // LOW
        rows = pl.ds(pl.multiple_of(g * depth, depth), depth)
        keys[0, rows, :] = (key - upper * LOW).astype(jnp.float32)
        keys[1, rows, :] = upper.astype(jnp.float32)
        return carry

    lax.fori_loop(0, index_ref.shape[0], block, 0)


def products(table_ref, lines_ref, prod, parity):
    half = table_ref.shape[1]

    def group(f, carry):
        right = lines_ref[f, :, parity].reshape(half, lines_ref.shape[-1])

        def rows_of(i, inner):
            rows = pl.ds(pl.multiple_of(i * 256, 256), 256)
            prod[f, parity, rows, :] = jnp.dot(
                table_ref[parity, rows, :], right, preferred_element_type=jnp.float32
            )
            return inner

        return lax.fori_loop(0, half // 256, rows_of, carry)

    lax.fori_loop(0, prod.shape[0], group, 0)


def local_kernel(length, table_ref, lines_ref, index_ref, wave_ref, out_ref, prod, vals, keys):
    unpack(index_ref, keys)
    products(table_ref, lines_ref, prod, 0)
    products(table_ref, lines_ref, prod, 1)
    bins(length, wave_ref, out_ref, prod, vals, keys)


def exchange_kernel(
    length, field_count, gz_count, table_ref, lines_ref, index_ref, wave_ref, out_ref,
    prod, vals, keys, lines, index, send, recv, own, index_send, index_recv, index_own,
):
    devices = field_count * gz_count
    me_field, me_gz = lax.axis_index("field"), lax.axis_index("gz")
    far = gz_count // 2
    mine = (gz_count - far) * field_count

    def peer(step):
        f = lax.rem(me_field + lax.rem(step, field_count), field_count)
        g = lax.rem(me_gz + step // field_count + far, gz_count)
        return f, g

    def others(run):
        def loop(step, carry):
            run(step)
            return carry

        lax.fori_loop(0, mine, loop, 0)
        lax.fori_loop(mine + 1, devices, loop, 0)

    def along(run):
        def loop(step, carry):
            run(step)
            return carry

        lax.fori_loop(1, gz_count, loop, 0)

    barrier = pltpu.get_barrier_semaphore()
    others(
        lambda step: pl.semaphore_signal(
            barrier, inc=1, device_id=peer(step), device_id_type=pl.DeviceIdType.MESH
        )
    )
    pl.semaphore_wait(barrier, devices - 1)

    def index_copy(step):
        g = lax.rem(me_gz + step, gz_count)
        return pltpu.make_async_remote_copy(
            src_ref=index_ref.at[g],
            dst_ref=index.at[me_gz],
            send_sem=index_send.at[step],
            recv_sem=index_recv.at[step],
            device_id=(me_field, g),
            device_id_type=pl.DeviceIdType.MESH,
        )

    def lines_copy(parity):
        def copy(step):
            f, g = peer(step)
            return pltpu.make_async_remote_copy(
                src_ref=lines_ref.at[f * gz_count + g, parity],
                dst_ref=lines.at[me_field, me_gz, parity],
                send_sem=send.at[parity, step],
                recv_sem=recv.at[parity, step],
                device_id=(f, g),
                device_id_type=pl.DeviceIdType.MESH,
            )

        return copy

    along(lambda step: index_copy(step).start())
    for parity in range(2):
        others(lambda step: lines_copy(parity)(step).start())
    me = me_field * gz_count + me_gz
    kept = [
        pltpu.make_async_copy(
            lines_ref.at[me, parity], lines.at[me_field, me_gz, parity], own.at[parity]
        )
        for parity in range(2)
    ]
    kept_index = pltpu.make_async_copy(index_ref.at[me_gz], index.at[me_gz], index_own)
    for copy in kept + [kept_index]:
        copy.start()

    kept_index.wait()
    along(lambda step: index_copy(step).wait_recv())
    unpack(index, keys)
    for parity in range(2):
        kept[parity].wait()
        others(lambda step: lines_copy(parity)(step).wait_recv())
        products(table_ref, lines, prod, parity)
    bins(length, wave_ref, out_ref, prod, vals, keys)
    along(lambda step: index_copy(step).wait_send())
    for parity in range(2):
        others(lambda step: lines_copy(parity)(step).wait_send())


def bins(length, wave_ref, out_ref, prod, vals, keys):
    quarter, half = length // 4, length // 2
    groups, local = prod.shape[0], prod.shape[3] // (2 * LANES)
    fields = groups * local
    out_ref[...] = jnp.zeros_like(out_ref)
    wave_x = wave_ref[0:1, :]
    wave_y = wave_ref[1:2, :]
    low_iota = lax.broadcasted_iota(jnp.int32, (16, LANES), 0).astype(jnp.float32)
    iotas = [(low_iota + 16.0 * j).astype(jnp.bfloat16) for j in range(LANES // 16)]
    one = jnp.ones((16, LANES), jnp.bfloat16)
    none = jnp.zeros((16, LANES), jnp.bfloat16)

    def cell_row(j, k):
        start = 1 - (k + quarter - 1) // quarter
        return (
            k,
            half - k,
            half + k - quarter * start,
            length - k - quarter * start,
        )[j]

    def tile(t, carry):
        first = pl.multiple_of(t * 8, 8)
        row = lax.broadcasted_iota(jnp.int32, (8, LANES), 0) + first
        special = row == 0

        def load(a, c, parity, sine):
            g, i = a // local, a % local
            at = (c * local + i) * LANES
            return prod[g, parity, pl.ds(sine * quarter + first, 8), at : at + LANES]

        def spectra(a):
            parts = []
            for c in range(2):
                ec, oc = load(a, c, 0, 0), load(a, c, 1, 0)
                es, os = load(a, c, 0, 1), load(a, c, 1, 1)
                p, q, m, n = ec + oc, es + os, ec - oc, os - es
                parts.append(
                    (
                        (p, jnp.where(special, 0.0, q)),
                        (m, jnp.where(special, 0.0, n)),
                        (jnp.where(special, es, m), jnp.where(special, os, -n)),
                        (jnp.where(special, es, p), jnp.where(special, -os, -q)),
                    )
                )
            u, v = parts
            return [(u[j][0] + v[j][1], v[j][0] - u[j][1]) for j in range(4)]

        k = row.astype(jnp.float32)
        zero_wave = (0.0, -half, quarter, -quarter)
        waves = (k, half - k, k - half, -k)
        base = spectra(0)
        second = None
        totals = [None] * 4
        saved = [None] * 4
        pending = [None] * 4
        for a in range(fields):
            spec = base if a == 0 else spectra(a)
            for j in range(4):
                cross = base[j][0] * spec[j][0] + base[j][1] * spec[j][1]
                if a == 0:
                    wz = jnp.where(special, float(zero_wave[j]), waves[j])
                    square = wave_x * wave_x + wave_y * wave_y + wz * wz
                    saved[j] = (wz, 1.0 / square)
                    vals[0, j * 8 : j * 8 + 8] = round16(cross)
                    continue
                wz, inverse = saved[j]
                if a == 1:
                    vals[1, j * 8 : j * 8 + 8] = round16(cross)
                    term = -0.5 * cross
                else:
                    weight = (
                        1.5 * wave_x * wave_x,
                        1.5 * wave_y * wave_y,
                        1.5 * wz * wz,
                        3.0 * wave_x * wave_y,
                        3.0 * wave_x * wz,
                        3.0 * wave_y * wz,
                    )[a - 2]
                    term = weight * inverse * cross
                pending[j] = term if pending[j] is None else pending[j] + term
                if a % local == local - 1:
                    rounded = round16(pending[j])
                    totals[j] = rounded if totals[j] is None else totals[j] + rounded
                    pending[j] = None
        for j in range(4):
            high = round16(totals[j])
            vals[2, j * 8 : j * 8 + 8] = high
            vals[3, j * 8 : j * 8 + 8] = totals[j] - high
        total = out_ref[...]
        for start in range(0, 32, PAIRS):
            left, hot = [], []
            for r in range(start, start + PAIRS):
                cell = cell_row(r // 8, first + r % 8)
                spread = [
                    jnp.broadcast_to(part, (16, LANES)).astype(jnp.bfloat16)
                    for part in [vals[i, r : r + 1] for i in range(4)]
                    + [keys[i, pl.ds(cell, 1), :] for i in range(2)]
                ]
                match = spread[4] == iotas[0]
                left.append(
                    jnp.concatenate(
                        [jnp.where(match, spread[i], none) for i in range(4)]
                        + [jnp.where(match, one, none)],
                        axis=0,
                    )
                )
                hot.append(
                    jnp.concatenate(
                        [jnp.where(spread[5] == it, one, none) for it in iotas], axis=0
                    )
                )
            total = total + lax.dot_general(
                jnp.concatenate(left, axis=1),
                jnp.concatenate(hot, axis=1),
                (((1,), (1,)), ((), ())),
                preferred_element_type=jnp.float32,
            )
        out_ref[...] = total
        return carry

    lax.fori_loop(0, quarter // 8, tile, 0)


def relayout_kernel(fields_ref, out_ref):
    for c in range(2):
        for i in range(fields_ref.shape[2]):
            at = (c * fields_ref.shape[2] + i) * LANES
            for h in range(out_ref.shape[1]):
                block = fields_ref[:, c, i, :, h * LANES : (h + 1) * LANES]
                block = block.reshape(16, 2, block.shape[1], LANES)
                for parity in range(2):
                    out_ref[:, h, parity, :, at : at + LANES] = jnp.swapaxes(
                        block[:, parity], 0, 1
                    )


def relayout(fields):
    depth, _, local, planes, yrows = fields.shape
    parts = yrows // LANES
    out = pl.pallas_call(
        relayout_kernel,
        grid=(depth // 32,),
        out_shape=jax.ShapeDtypeStruct(
            (planes, parts, 2, depth // 2, 2 * local * LANES), fields.dtype
        ),
        in_specs=[pl.BlockSpec((32, 2, local, planes, yrows), lambda i: (i, 0, 0, 0, 0))],
        out_specs=pl.BlockSpec(
            (planes, parts, 2, 16, 2 * local * LANES), lambda i: (0, 0, 0, i, 0)
        ),
    )(fields)
    return out.reshape(planes * parts, 2, depth // 2, 2 * local * LANES)


def reduce_kernel(field_count, gz_count, mine_ref, out_ref, parts, answer, send, recv, send2, recv2):
    devices = field_count * gz_count
    me_field, me_gz = lax.axis_index("field"), lax.axis_index("gz")
    me = me_field * gz_count + me_gz

    def peer(step):
        other = lax.rem(me + step, devices)
        return other, (other // gz_count, lax.rem(other, gz_count))

    barrier = pltpu.get_barrier_semaphore()

    def greet(step, carry):
        _, place = peer(step)
        pl.semaphore_signal(
            barrier, inc=1, device_id=place, device_id_type=pl.DeviceIdType.MESH
        )
        return carry

    lax.fori_loop(1, devices, greet, 0)
    pl.semaphore_wait(barrier, devices - 1)

    def scatter(step):
        other, place = peer(step)
        return pltpu.make_async_remote_copy(
            src_ref=mine_ref.at[other],
            dst_ref=parts.at[step],
            send_sem=send.at[step],
            recv_sem=recv.at[step],
            device_id=place,
            device_id_type=pl.DeviceIdType.MESH,
        )

    def gather(step):
        _, place = peer(step)
        return pltpu.make_async_remote_copy(
            src_ref=answer,
            dst_ref=out_ref.at[me],
            send_sem=send2.at[step],
            recv_sem=recv2.at[step],
            device_id=place,
            device_id_type=pl.DeviceIdType.MESH,
        )

    def start(copy):
        def run(step, carry):
            copy(step).start()
            return carry

        lax.fori_loop(1, devices, run, 0)

    start(scatter)

    def collect(step, total):
        scatter(step).wait_recv()
        return total + parts[step]

    answer[...] = lax.fori_loop(1, devices, collect, mine_ref[me])
    start(gather)
    out_ref[me] = answer[...]

    def finish(step, carry):
        scatter(step).wait_send()
        gather(step).wait()
        return carry

    lax.fori_loop(1, devices, finish, 0)


def all_reduce(total, field_count, gz_count):
    devices = field_count * gz_count
    rows = max(1, total.shape[0] // devices)
    total = jnp.pad(total, ((0, devices * rows - total.shape[0]), (0, 0)))
    total = total.reshape(devices, rows, LANES)
    return pl.pallas_call(
        functools.partial(reduce_kernel, field_count, gz_count),
        out_shape=jax.ShapeDtypeStruct(total.shape, jnp.float32),
        in_specs=[pl.BlockSpec(memory_space=pltpu.VMEM)],
        out_specs=pl.BlockSpec(memory_space=pltpu.VMEM),
        scratch_shapes=[
            pltpu.VMEM(total.shape, jnp.float32),
            pltpu.VMEM(total.shape[1:], jnp.float32),
            pltpu.SemaphoreType.DMA((devices,)),
            pltpu.SemaphoreType.DMA((devices,)),
            pltpu.SemaphoreType.DMA((devices,)),
            pltpu.SemaphoreType.DMA((devices,)),
        ],
        compiler_params=pltpu.CompilerParams(collective_id=0, has_side_effects=True),
    )(total).reshape(devices * rows, LANES)


def body(fields, shells, mubins):
    depth_local, _, local_fields, planes, yrows = fields.shape
    gz_count, field_count = lax.axis_size("gz"), lax.axis_size("field")
    devices = gz_count * field_count
    length = depth_local * gz_count
    half = length // 2
    plane_rows = planes * yrows
    width = plane_rows // devices
    me_gz, me_field = lax.axis_index("gz"), lax.axis_index("field")

    exchange = width == LANES and depth_local % 32 == 0
    if exchange:
        lines = relayout(fields)
    else:
        lines = fields.reshape(depth_local // 2, 2, 2, local_fields, devices, width)
        lines = lines.transpose(4, 1, 0, 2, 3, 5).reshape(
            devices, 2, depth_local // 2, 2 * local_fields * width
        )

    share = planes // field_count
    shells, mubins = (
        lax.dynamic_slice_in_dim(ids, me_field * share, share, 1) for ids in (shells, mubins)
    )
    index = (shells + mubins * 65536).reshape(depth_local, gz_count, width).transpose(1, 0, 2)

    span = 2 * local_fields * LANES
    table = quarter_tables(length, jnp.minimum(me_gz, 0))
    column = (me_field * gz_count + me_gz) * width + jnp.arange(LANES, dtype=jnp.int32)
    waves = jnp.stack([length // 4 + column // yrows, length // 8 + column % yrows])
    waves = jnp.pad(waves.astype(jnp.float32), ((0, 6), (0, 0)))
    landed = (field_count, gz_count, 2, depth_local // 2, span)
    scratch = [
        pltpu.VMEM((field_count, 2, half, span), jnp.float32),
        pltpu.VMEM((4, 32, LANES), jnp.float32),
        pltpu.VMEM((2, length, LANES), jnp.float32),
    ]
    vmem, anywhere = pl.BlockSpec(memory_space=pltpu.VMEM), pl.BlockSpec(memory_space=pl.ANY)
    if exchange:
        run, places, wide = (
            functools.partial(exchange_kernel, length, field_count, gz_count),
            anywhere,
            dict(collective_id=1, has_side_effects=True),
        )
        scratch += [
            pltpu.VMEM(landed, jnp.bfloat16),
            pltpu.VMEM((gz_count, depth_local, LANES), jnp.int32),
            pltpu.SemaphoreType.DMA((2, devices)),
            pltpu.SemaphoreType.DMA((2, devices)),
            pltpu.SemaphoreType.DMA((2,)),
            pltpu.SemaphoreType.DMA((gz_count,)),
            pltpu.SemaphoreType.DMA((gz_count,)),
            pltpu.SemaphoreType.DMA,
        ]
    else:
        run, places, wide = functools.partial(local_kernel, length), vmem, {}
        lines = lax.all_to_all(lines, ("field", "gz"), split_axis=0, concat_axis=0, tiled=True)
        lines = lines.reshape(landed[:-1] + (2 * local_fields, width))
        lines = jnp.pad(lines, ((0, 0),) * 5 + ((0, LANES - width),)).reshape(landed)
        index = lax.all_to_all(index, "gz", split_axis=0, concat_axis=0, tiled=True)
        index = jnp.pad(index, ((0, 0), (0, 0), (0, LANES - width)), constant_values=SHELLS)

    total = pl.pallas_call(
        run,
        out_shape=jax.ShapeDtypeStruct((ROWS * LOW, LANES), jnp.float32),
        in_specs=[vmem, places, places, vmem],
        out_specs=vmem,
        scratch_shapes=scratch,
        compiler_params=pltpu.CompilerParams(vmem_limit_bytes=56 * 1024 * 1024, **wide),
    )(table, lines, index, waves)

    total = total.reshape(ROWS, LOW, LANES)
    total = jnp.concatenate([total[:2], total[2:3] + total[3:4], total[4:]])
    total = all_reduce(total.reshape(-1, LANES), field_count, gz_count)[: 4 * LOW]
    total = total.reshape(4, 2, MUBINS, LANES).transpose(0, 2, 3, 1)
    total = total.reshape(4, MUBINS, SHELLS)
    return total[:3] / jnp.maximum(total[3], 1.0)[None]


def solution(mesh):
    in_specs = (P("gz", None, "field", None, None), P("gz", None, None), P("gz", None, None))
    return jax.shard_map(body, mesh=mesh, in_specs=in_specs, out_specs=P(), check_vma=False)
```

time: 310 us -> 295 us (0.952)
  Pallas kernels: 70.6 us -> 276 us
  waiting for transfers between devices: 147 us -> 0 us
  other arithmetic: 43.3 us -> 10.3 us
  blocking collectives: 32.7 us -> 0 us
  starting transfers between devices: 3.91 us -> 0 us
  local copies, waits for them, and re-layouts: 11.4 us -> 7.83 us
    pallas_call x1, Pallas kernels: 47.2 us -> 251 us  [body(): pl.pallas_call(run, out_shape=jax.ShapeDtypeStruct((ROWS * LOW, LANES), j...]
    all_to_all x1 -> x0, waiting for transfers between devices: 147 us -> none  [body(): lax.all_to_all(lines, ('field', 'gz'), split_axis=0, concat_axis=0, tiled...]
    all_to_all x1 -> x0, blocking collectives: 32.7 us -> none  [body(): lax.all_to_all(packed, 'gz', split_axis=0, concat_axis=0, tiled=True)]
    convert_element_type x1, other arithmetic: 32.9 us -> 0.78 us  [quarter_tables(): cos_part.astype(jnp.bfloat16)]
    add x3, other arithmetic: 7.15 us -> 0.15 us  [the longest x1 0.14 us: body(): shells + mubins * 65536]
    add x1 -> x0, local copies, waits for them, and re-layouts: 5.25 us -> none  [body(): packed = shells + mubins * 65536]
    all_to_all x1 -> x0, starting transfers between devices: 3.91 us -> none  [body(): lax.all_to_all(lines, ('field', 'gz'), split_axis=0, concat_axis=0, tiled...]
  transfers between devices with their start and end apart: 1 -> 0, of which waited for: 1 -> 0; matrix products, arithmetic and copies ran while one was open for 12% -> 0% of each run, Pallas kernels for 0% -> 0%
where the time goes in v3:
time: 295 us
  Pallas kernels  276 us (94%)
  other arithmetic  10.3 us (3%)
  local copies, waits for them, and re-layouts  7.83 us (3%)
    pallas_call x1, Pallas kernels, body(): pl.pallas_call(run, out_shape=jax.ShapeDtypeStruct((ROWS * LOW, LANES), j...  251 us
    pallas_call x1, Pallas kernels, all_reduce(): pl.pallas_call(functools.partial(reduce_kernel, field_count, gz_count), o...  15.9 us
    pallas_call x1, Pallas kernels, relayout(): pl.pallas_call(relayout_kernel, grid=(depth // 32,), out_shape=jax.ShapeD...  9.87 us

profile of v3, /device:TPU:0, one launch (start us, length us, event | category | flops | bytes accessed | tf_op | source)
XLA Modules:
  0.0 294.6 jit_solution(10308597897548692869)
XLA Ops:
  0.1 0.6 pad.4.wave_ref
  0.7 1.2 fusion.9
  1.9 1.8 fusion.4
  3.8 2.6 constant_dynamic-slice_fusion
  6.3 0.4 copy.11
  6.7 0.4 copy.10
  7.1 0.1 multiply_add_fusion
  7.3 0.0 copy-start
  7.3 0.0 copy-start.1
  7.3 1.4 copy.7
  8.7 1.9 add_multiply_fusion
  10.6 0.5 fusion
  11.1 0.0 copy-done
  11.1 0.8 multiply_convert_fusion
  11.9 2.4 pad_maximum_fusion.table_ref
  14.3 9.9 %shard_map.37 = bf16[16,2,2,128,512]{4,3,2,1,0:T(8,128)(2,1)} custom-call(bf16[256,2,2,16,256]{4,3,2,1,0:T(8,128)(2,1)} %fields_ref.1), custom_call_target="tpu_custom_call" | custom-call | tf_op jit(solution)/shard_map/pallas_call | solution.py:321
  24.2 250.5 %shard_map.38 = f32[80,128]{1,0:T(8,128)} custom-call(bf16[2,1024,1024]{2,1,0:T(8,128)(2,1)} %pad_maximum_fusion.table_ref, bf16[32,2,128,512]{3,2,1,0:T(8,128)(2,1)} %bitcast.18, s32[8,256,128]{2,1,0:T(8,128)} %bitcast.21, f32[8,128]{1,0:T(8,128)} %pad.4.wave_ref), custom_call_target="tpu_custom_call" | custom-call | tf_op jit(solution)/shard_map/pallas_call | solution.py:486
  274.7 0.7 slice.30
  275.5 0.7 add_bitcast_fusion
  276.2 0.6 pad_maximum_fusion.1
  276.8 15.9 %shard_map.39 = f32[32,2,128]{2,1,0:T(2,128)} custom-call(f32[32,2,128]{2,1,0:T(2,128)} %bitcast.27), custom_call_target="tpu_custom_call" | custom-call | tf_op jit(solution)/shard_map/pallas_call | solution.py:408
  292.7 1.0 copy.8
  293.7 0.1 slice_maximum_fusion
  293.8 0.7 copy.9
  (11 shorter events, 0.1 us)
Async XLA Ops:
  7.3 3.8 %copy-start = (f32[2,32,1024]{2,1,0:T(8,128)S(1)}, f32[2,32,1024]{2,1,0:T(8,128)}, u32[]{:S(2)}) copy-start(f32[2,32,1024]{2,1,0:T(8,128)} %get-tuple-element.9) | copy-start | bytes 786436
  7.3 3.8 %copy-start.1 = (f32[2,16,1024]{2,1,0:T(8,128)S(1)}, f32[2,16,1024]{2,1,0:T(8,128)}, u32[]{:S(2)}) copy-start(f32[2,16,1024]{2,1,0:T(8,128)} %get-tuple-element.10) | copy-start | bytes 393220

commit v4 on v3

--- a/solution.py
+++ b/solution.py
@@ -14,7 +14,7 @@
 LANES = 128
 LOW = 16
 ROWS = 5
-PAIRS = 8
+PAIRS = 32
 
 
 def quarter_tables(length, zero):

time: 295 us -> 299 us (1.014)
  Pallas kernels: 276 us -> 281 us
    pallas_call x1, Pallas kernels: 251 us -> 255 us  [body(): pl.pallas_call(run, out_shape=jax.ShapeDtypeStruct((ROWS * LOW, LANES), j...]
where the time goes in v4:
time: 299 us
  Pallas kernels  281 us (94%)
  other arithmetic  10.3 us (3%)
  local copies, waits for them, and re-layouts  7.83 us (3%)
    pallas_call x1, Pallas kernels, body(): pl.pallas_call(run, out_shape=jax.ShapeDtypeStruct((ROWS * LOW, LANES), j...  255 us
    pallas_call x1, Pallas kernels, all_reduce(): pl.pallas_call(functools.partial(reduce_kernel, field_count, gz_count), o...  15.9 us
    pallas_call x1, Pallas kernels, relayout(): pl.pallas_call(relayout_kernel, grid=(depth // 32,), out_shape=jax.ShapeD...  9.87 us

profile of v4, /device:TPU:0, one launch (start us, length us, event | category | flops | bytes accessed | tf_op | source)
XLA Modules:
  0.0 298.9 jit_solution(1879596362136162884)
XLA Ops:
  0.1 0.6 pad.4.wave_ref
  0.7 1.2 fusion.9
  1.9 1.8 fusion.4
  3.8 2.6 constant_dynamic-slice_fusion
  6.3 0.4 copy.11
  6.7 0.4 copy.10
  7.1 0.1 multiply_add_fusion
  7.3 0.0 copy-start
  7.3 0.0 copy-start.1
  7.3 1.4 copy.7
  8.7 1.9 add_multiply_fusion
  10.6 0.5 fusion
  11.1 0.0 copy-done
  11.1 0.8 multiply_convert_fusion
  11.9 2.4 pad_maximum_fusion.table_ref
  14.3 9.9 %shard_map.37 = bf16[16,2,2,128,512]{4,3,2,1,0:T(8,128)(2,1)} custom-call(bf16[256,2,2,16,256]{4,3,2,1,0:T(8,128)(2,1)} %fields_ref.1), custom_call_target="tpu_custom_call" | custom-call | tf_op jit(solution)/shard_map/pallas_call | solution.py:321
  24.2 254.8 %shard_map.38 = f32[80,128]{1,0:T(8,128)} custom-call(bf16[2,1024,1024]{2,1,0:T(8,128)(2,1)} %pad_maximum_fusion.table_ref, bf16[32,2,128,512]{3,2,1,0:T(8,128)(2,1)} %bitcast.18, s32[8,256,128]{2,1,0:T(8,128)} %bitcast.21, f32[8,128]{1,0:T(8,128)} %pad.4.wave_ref), custom_call_target="tpu_custom_call" | custom-call | tf_op jit(solution)/shard_map/pallas_call | solution.py:486
  279.0 0.7 slice.30
  279.8 0.7 add_bitcast_fusion
  280.5 0.6 pad_maximum_fusion.1
  281.1 15.9 %shard_map.39 = f32[32,2,128]{2,1,0:T(2,128)} custom-call(f32[32,2,128]{2,1,0:T(2,128)} %bitcast.27), custom_call_target="tpu_custom_call" | custom-call | tf_op jit(solution)/shard_map/pallas_call | solution.py:408
  297.0 1.0 copy.8
  298.0 0.1 slice_maximum_fusion
  298.1 0.7 copy.9
  (11 shorter events, 0.1 us)
Async XLA Ops:
  7.3 3.8 %copy-start = (f32[2,32,1024]{2,1,0:T(8,128)S(1)}, f32[2,32,1024]{2,1,0:T(8,128)}, u32[]{:S(2)}) copy-start(f32[2,32,1024]{2,1,0:T(8,128)} %get-tuple-element.9) | copy-start | bytes 786436
  7.3 3.8 %copy-start.1 = (f32[2,16,1024]{2,1,0:T(8,128)S(1)}, f32[2,16,1024]{2,1,0:T(8,128)}, u32[]{:S(2)}) copy-start(f32[2,16,1024]{2,1,0:T(8,128)} %get-tuple-element.10) | copy-start | bytes 393220
